TPU v7x, 512 devices: a whole 4x8x8 slice. The times are simulated.
512 devices in a mesh: shards: 16 (over z, core), tensor: 4 (over x), sections: 8 (over y).
Axes of the slice: x: 4, y: 8, z: 8, core: 2. Of those that a mesh axis runs over, the one named last changes fastest.
Arguments:
- replica_grads: bfloat16 [16, 8, 2, 1536, 512], P('shards', 'sections', None, None, 'tensor'), may hold values from -6 to 6
- error_feedback: bfloat16 [16, 8, 2, 1536, 512], P('shards', 'sections', None, None, 'tensor'), may hold values from -3 to 3
- q_start: float32 [8, 2, 512, 32], P('sections', None, 'tensor'), may hold values from -0.25 to 0.25
- gram_root: float32 [8, 2, 32, 32], P('sections'), may hold values from -2 to 2
- momentum: float32 [8, 2, 1536, 512], P('sections', None, 'shards', 'tensor'), may hold values from -1.2 to 1.2
- weights: float32 [8, 2, 1536, 512], P('sections', None, 'shards', 'tensor'), may hold values from -3 to 3
- router_partials: bfloat16 [512, 1536, 40], P(('shards', 'tensor', 'sections')), may hold values from -12 to 12
- gain_partials: bfloat16 [512, 2, 1536], P(('shards', 'tensor', 'sections')), may hold values from -12 to 12
- router_momentum: float32 [1536, 40], P('shards'), may hold values from -1.2 to 1.2
- router_weights: float32 [1536, 40], P('shards'), may hold values from -3 to 3
- gain_momentum: float32 [2, 1536], P(None, 'shards'), may hold values from -1.2 to 1.2
- gain_weights: float32 [2, 1536], P(None, 'shards'), may hold values from 0.1 to 1.9
Outputs:
- new_error: bfloat16 [16, 8, 2, 1536, 512], P('shards', 'sections', None, None, 'tensor')
- new_momentum: float32 [8, 2, 1536, 512], P('sections', None, 'shards', 'tensor')
- new_weights: float32 [8, 2, 1536, 512], P('sections', None, None, 'tensor')
- new_router_momentum: float32 [1536, 40], P('shards')
- new_router_weights: float32 [1536, 40], replicated
- new_gain_momentum: float32 [2, 1536], P(None, 'shards')
- new_gain_weights: float32 [2, 1536], replicated
All inputs are finite; a program needn't handle non-finite values.
Results may differ from a plain program's by a relative error of at most 0.001.
Values sent between devices are 32-bit elements; how exact they have to be, the bound alone decides.
No kernel may reach another device: no remote copies, remote signals or barrier semaphores. Data moves between devices by JAX's collectives and lax.ppermute only.
A program may use at most 64 MiB of HBM per device.

v0:
```python
import jax
import jax.numpy as jnp
from jax import lax
from jax.sharding import PartitionSpec as P

momentum_decay = 0.9
step_size = 0.5
lanes = 128
rank = 32
highest = lax.Precision.HIGHEST
f32 = jnp.float32
plane = ("shards", "tensor")
sheet = ("tensor", "sections")


def exchange(blocks, axes):
    return lax.all_to_all(blocks, axes, 0, 0, tiled=True)


def spread(row, count, axes):
    return exchange(jnp.broadcast_to(row, (count,) + row.shape[1:]), axes)


def per_device(
    replica_grads,
    error_feedback,
    q_start,
    gram_root,
    momentum,
    weights,
    router_partials,
    gain_partials,
    router_momentum,
    router_weights,
    gain_momentum,
    gain_weights,
):
    shard_count = lax.axis_size("shards")
    tensor_count = lax.axis_size("tensor")
    section_count = lax.axis_size("sections")
    plane_count = shard_count * tensor_count
    sheet_count = tensor_count * section_count
    shard_index = lax.axis_index("shards")
    rows = momentum.shape[2]
    width = gain_partials.shape[2]
    start = shard_index * rows
    blocks = width // lanes
    base_rows = weights[0] - step_size * momentum_decay * momentum[0]
    base = lax.all_gather(base_rows, "shards", axis=1, tiled=True)
    columns = jnp.concatenate([router_partials[0].T, gain_partials[0]], 0).astype(f32)
    count = columns.shape[0]
    strips = columns.reshape(count, blocks, lanes).transpose(1, 0, 2).reshape(count * blocks, lanes)
    total_rows = plane_count * section_count
    strips = jnp.pad(strips, ((0, total_rows - count * blocks), (0, 0)))
    strips = strips.reshape(tensor_count, section_count, shard_count, lanes).transpose(1, 2, 0, 3)
    strips = strips.reshape(section_count, plane_count, lanes)
    strips = exchange(strips, "sections").sum(0)
    combined = replica_grads[0, 0].astype(f32) + error_feedback[0, 0].astype(f32)
    q_rows = q_start[0].transpose(0, 2, 1)
    p_rows = jnp.einsum("krf,kdf->krd", q_rows, combined, precision=highest)
    p_row = exchange(p_rows.reshape(plane_count, width), plane).sum(0, keepdims=True)
    packed = jnp.concatenate([jnp.broadcast_to(p_row, (plane_count, width)), strips], 1)
    packed = exchange(packed, plane)
    strip = packed[:, width:].sum(0, keepdims=True)
    p_avg = packed[:, :width].reshape(2, rank, width) / shard_count
    p_hat = jnp.einsum("krd,krt->ktd", p_avg, gram_root[0], precision=highest)
    q_local = jnp.einsum("ktd,kdf->ktf", p_hat, combined, precision=highest)
    small_base = jnp.concatenate(
        [
            router_weights.T - step_size * momentum_decay * router_momentum.T,
            gain_weights - step_size * momentum_decay * gain_momentum,
        ],
        0,
    )
    small_base = jnp.pad(small_base, ((0, 48 - count), (0, lanes - rows)))
    bundle = jnp.concatenate(
        [q_local.reshape(2 * rank, lanes), small_base, jnp.pad(strip, ((0, 7), (0, 0)))], 0
    )
    bundle = lax.all_gather(bundle, "shards", axis=0, tiled=False)
    q_avg = (bundle[:, : 2 * rank].sum(0) / shard_count).reshape(2, rank, lanes)
    strip_set = bundle[:, 2 * rank + 48]
    small_base = (
        bundle[:, 2 * rank : 2 * rank + count, :rows].transpose(1, 0, 2).reshape(count, width)
    )
    small = spread(strip_set[None], sheet_count, sheet)
    small = small.reshape(total_rows, lanes)[: count * blocks]
    small = (
        small.reshape(blocks, count, lanes).transpose(1, 0, 2).reshape(count, width) / shard_count
    )
    approx = jnp.einsum("ktd,ktf->kdf", p_hat, q_avg, precision=highest)
    new_error = (combined - approx).astype(jnp.bfloat16)[None, None]
    new_weights = (base - step_size * approx)[None]
    approx_rows = lax.dynamic_slice_in_dim(approx, start, rows, 1)
    new_momentum = momentum_decay * momentum + approx_rows[None]
    own = lax.dynamic_slice_in_dim(small, start, rows, 1)
    new_router_momentum = momentum_decay * router_momentum + own[:-2].T
    new_gain_momentum = momentum_decay * gain_momentum + own[-2:]
    new_small = small_base - step_size * small
    return (
        new_error,
        new_momentum,
        new_weights,
        new_router_momentum,
        new_small[:-2].T,
        new_gain_momentum,
        new_small[-2:],
    )


def solution(mesh):
    return jax.shard_map(
        per_device,
        mesh=mesh,
        in_specs=(
            P("shards", "sections", None, None, "tensor"),
            P("shards", "sections", None, None, "tensor"),
            P("sections", None, "tensor", None),
            P("sections", None, None, None),
            P("sections", None, "shards", "tensor"),
            P("sections", None, "shards", "tensor"),
            P(("shards", "tensor", "sections"), None, None),
            P(("shards", "tensor", "sections"), None, None),
            P("shards", None),
            P("shards", None),
            P(None, "shards"),
            P(None, "shards"),
        ),
        out_specs=(
            P("shards", "sections", None, None, "tensor"),
            P("sections", None, "shards", "tensor"),
            P("sections", None, None, "tensor"),
            P("shards", None),
            P(),
            P(None, "shards"),
            P(),
        ),
        check_vma=False,
    )
```

profile of v0, /device:TPU:1, one launch (start us, length us, event | category | flops | bytes accessed | tf_op | source)
XLA Modules:
  0.0 150.9 jit_solution(3413235072184591693)
XLA Ops:
  8.0 1.0 concatenate.17
  10.0 7.7 %all-to-all-start.1 = ((f32[8,64,128]{2,1,0:T(8,128)}), f32[8,64,128]{2,1,0:T(8,128)S(1)}, u32[]{:S(2)}, u32[]{:S(2)}) async-start(f32[8,64,128]{2,1,0:T(8,128)} %copy.30), calls=%async_computation.1 | async-start | bytes 524288 | tf_op jit(solution)/shard_map/all_to_all | solution.py:17
  17.6 1.8 %fusion.3 = f32[2,1536,32]{1,2,0:T(8,128)S(1)} fusion(bf16[1,1,2,1536,128]{4,3,2,1,0:T(8,128)(2,1)S(1)} %copy-done.1, bf16[1,1,2,1536,128]{4,3,2,1,0:T(8,128)(2,1)S(1)} %copy-done.2, f32[1,2,128,32]{2,3,1,0:T(8,128)S(1)} %copy-done), kind=kOutput, calls=%fused_computation.5 | convolution fusion | flops 152174592 | bytes 1998848 | tf_op jit(solution)/shard_map/krf,kdf->krd/dot_general | solution.py:60
  19.5 1.2 copy.27
  20.6 6.4 %all-to-all-done.1 = f32[8,64,128]{2,1,0:T(8,128)S(1)} async-done(((f32[8,64,128]{2,1,0:T(8,128)}), f32[8,64,128]{2,1,0:T(8,128)S(1)}, u32[]{:S(2)}, u32[]{:S(2)}) %all-to-all-start.1) | async-done | bytes 262176 | tf_op jit(solution)/shard_map/all_to_all | solution.py:17
  27.0 16.8 %all-to-all-start = ((f32[64,1,1536]{2,1,0:T(1,128)}), f32[64,1,1536]{2,1,0:T(1,128)S(1)}, u32[]{:S(2)}, u32[]{:S(2)}) async-start(f32[64,1,1536]{2,1,0:T(1,128)} %copy.27), calls=%async_computation | async-start | bytes 786432 | tf_op jit(solution)/shard_map/all_to_all | solution.py:17
  43.9 14.6 %all-to-all-done = f32[64,1,1536]{2,1,0:T(1,128)S(1)} async-done(((f32[64,1,1536]{2,1,0:T(1,128)}), f32[64,1,1536]{2,1,0:T(1,128)S(1)}, u32[]{:S(2)}, u32[]{:S(2)}) %all-to-all-start) | async-done | bytes 393248 | tf_op jit(solution)/shard_map/all_to_all | solution.py:17
  58.7 1.1 all_to_all.23
  59.8 6.0 %all-to-all-start.2 = ((f32[64,1,1664]{2,1,0:T(1,128)}), f32[64,1,1664]{2,1,0:T(1,128)S(1)}, u32[]{:S(2)}, u32[]{:S(2)}) async-start(f32[64,1,1664]{2,1,0:T(1,128)} %all_to_all.23), calls=%async_computation.2 | async-start | bytes 851968 | tf_op jit(solution)/shard_map/all_to_all | solution.py:17
  65.9 15.3 %all-to-all-done.2 = f32[64,1,1664]{2,1,0:T(1,128)S(1)} async-done(((f32[64,1,1664]{2,1,0:T(1,128)}), f32[64,1,1664]{2,1,0:T(1,128)S(1)}, u32[]{:S(2)}, u32[]{:S(2)}) %all-to-all-start.2) | async-done | bytes 426016 | tf_op jit(solution)/shard_map/all_to_all | solution.py:17
  81.8 1.1 fusion.1
  82.9 19.7 %all-gather = f32[1920,128]{1,0:T(8,128)S(1)} all-gather(f32[120,128]{1,0:T(8,128)S(1)} %select_maximum_fusion), channel_id=2, replica_groups=mesh['shards'=16,'tensor'=4,'sections'=8] {'shards'}, dimensions={0}, use_global_device_ids=true | all-gather | bytes 1044480 | tf_op jit(solution)/shard_map/all_gather | solution.py:79
  102.6 0.9 copy-done.3
  103.5 2.6 %fusion.11 = f32[2,1536,128]{2,1,0:T(8,128)S(1)} fusion(f32[2,1536,32]{1,2,0:T(8,128)S(1)} %fusion.7, f32[2,32,128]{2,1,0:T(8,128)S(1)} %bitcast.89), kind=kOutput, calls=%fused_computation.36 | convolution fusion | flops 150994944 | bytes 1998848 | tf_op jit(solution)/shard_map/ktd,ktf->kdf/dot_general | solution.py:90
  108.4 4.6 %all-to-all-start.3 = ((f32[32,16,128]{2,1,0:T(8,128)}), f32[32,16,128]{2,1,0:T(8,128)}, u32[]{:S(2)}, u32[]{:S(2)}) async-start(f32[32,16,128]{2,1,0:T(8,128)} %broadcast_in_dim.31), calls=%async_computation.3 | async-start | bytes 524288 | tf_op jit(solution)/shard_map/all_to_all | solution.py:17
  113.0 1.0 slice.45
  114.2 0.9 reshape.78
  115.1 8.4 %all-to-all-done.3 = f32[32,16,128]{2,1,0:T(8,128)} async-done(((f32[32,16,128]{2,1,0:T(8,128)}), f32[32,16,128]{2,1,0:T(8,128)}, u32[]{:S(2)}, u32[]{:S(2)}) %all-to-all-start.3) | async-done | bytes 262176 | tf_op jit(solution)/shard_map/all_to_all | solution.py:17
  123.5 1.8 %slice_multiply_fusion.1 = (f32[504,128]{1,0:T(8,128)}, f32[504,128]{1,0:T(8,128)}) fusion(f32[512,128]{1,0:T(8,128)} %bitcast.22), kind=kLoop, calls=%fused_computation.16 | loop fusion | flops 129024 | bytes 774144 | tf_op jit(solution)/shard_map/mul | solution.py:98
  125.3 1.7 %mul.77 = f32[12,42,128]{2,1,0:T(8,128)} reshape(f32[504,128]{1,0:T(8,128)} %get-tuple-element.9) | data formatting | bytes 516096 | tf_op jit(solution)/shard_map/mul | solution.py:98
  127.0 1.1 copy.34
  129.0 1.0 div.36
  132.2 8.7 %all-gather.4.cloned.1.call-done = f32[1,2,1536,128]{3,2,1,0:T(8,128)} async-done(((f32[1,2,96,128]{3,2,1,0:T(8,128)}), f32[1,2,1536,128]{3,2,1,0:T(8,128)}) %all-gather.4.cloned.1.call-update) | async-done | bytes 1572880 | tf_op jit(solution)/shard_map/all_gather | solution.py:49
  140.9 3.2 %fusion = (f32[1,2,1536,128]{3,2,1,0:T(8,128)}, bf16[1,1,2,1536,128]{4,3,2,1,0:T(8,128)(2,1)}) fusion(f32[1,2,1536,128]{3,2,1,0:T(8,128)} %all-gather.4.cloned.1.call-done, f32[2,1536,128]{2,1,0:T(8,128)S(1)} %fusion.11, bf16[1,1,2,1536,128]{4,3,2,1,0:T(8,128)(2,1)S(1)} %copy-done.1, bf16[1,1,2,1536,128]{4,3,2,1,0:T(8,128)(2,1)S(1)} %copy-done.2), kind=kLoop, calls=%fused_computation.1 | loop fusion | flops 2752512 | bytes 7077888 | tf_op jit(solution)/shard_map/broadcast_in_dim | solution.py:92
  (64 shorter events, 8.3 us)
Async XLA Ops:
  7.2 10.5 %copy-start = (f32[1,2,128,32]{2,3,1,0:T(8,128)S(1)}, f32[1,2,128,32]{2,3,1,0:T(8,128)}, u32[]{:S(2)}) copy-start(f32[1,2,128,32]{2,3,1,0:T(8,128)} %param.14) | copy-start | bytes 98308
  7.2 10.4 %copy-start.1 = (bf16[1,1,2,1536,128]{4,3,2,1,0:T(8,128)(2,1)S(1)}, bf16[1,1,2,1536,128]{4,3,2,1,0:T(8,128)(2,1)}, u32[]{:S(2)}) copy-start(bf16[1,1,2,1536,128]{4,3,2,1,0:T(8,128)(2,1)} %param.13) | copy-start | bytes 2359300
  7.2 10.4 %copy-start.2 = (bf16[1,1,2,1536,128]{4,3,2,1,0:T(8,128)(2,1)S(1)}, bf16[1,1,2,1536,128]{4,3,2,1,0:T(8,128)(2,1)}, u32[]{:S(2)}) copy-start(bf16[1,1,2,1536,128]{4,3,2,1,0:T(8,128)(2,1)} %param.12) | copy-start | bytes 2359300
  10.0 17.1 %all-to-all-start.1 = ((f32[8,64,128]{2,1,0:T(8,128)}), f32[8,64,128]{2,1,0:T(8,128)S(1)}, u32[]{:S(2)}, u32[]{:S(2)}) async-start(f32[8,64,128]{2,1,0:T(8,128)} %copy.30), calls=%async_computation.1 | async-start | bytes 524288 | tf_op jit(solution)/shard_map/all_to_all | solution.py:17
  27.0 31.4 %all-to-all-start = ((f32[64,1,1536]{2,1,0:T(1,128)}), f32[64,1,1536]{2,1,0:T(1,128)S(1)}, u32[]{:S(2)}, u32[]{:S(2)}) async-start(f32[64,1,1536]{2,1,0:T(1,128)} %copy.27), calls=%async_computation | async-start | bytes 786432 | tf_op jit(solution)/shard_map/all_to_all | solution.py:17
  43.8 22.0 %copy-start.12 = (f32[2,96]{1,0:T(2,128)S(1)}, f32[2,96]{1,0:T(2,128)}, u32[]{:S(2)}) copy-start(f32[2,96]{1,0:T(2,128)} %param.22) | copy-start | bytes 2308
  43.8 22.0 %copy-start.13 = (f32[2,96]{1,0:T(2,128)S(1)}, f32[2,96]{1,0:T(2,128)}, u32[]{:S(2)}) copy-start(f32[2,96]{1,0:T(2,128)} %param.23) | copy-start | bytes 2308
  43.8 22.0 %copy-start.9 = (f32[96,40]{0,1:T(8,128)S(1)}, f32[96,40]{0,1:T(8,128)}, u32[]{:S(2)}) copy-start(f32[96,40]{0,1:T(8,128)} %param.20) | copy-start | bytes 46084
  43.8 22.0 %copy-start.11 = (f32[96,40]{0,1:T(8,128)S(1)}, f32[96,40]{0,1:T(8,128)}, u32[]{:S(2)}) copy-start(f32[96,40]{0,1:T(8,128)} %param.21) | copy-start | bytes 46084
  58.7 22.5 %copy-start.10 = (f32[1,2,32,32]{3,2,1,0:T(8,128)S(1)}, f32[1,2,32,32]{3,2,1,0:T(8,128)}, u32[]{:S(2)}) copy-start(f32[1,2,32,32]{3,2,1,0:T(8,128)} %param.15) | copy-start | bytes 24580
  59.8 21.4 %all-to-all-start.2 = ((f32[64,1,1664]{2,1,0:T(1,128)}), f32[64,1,1664]{2,1,0:T(1,128)S(1)}, u32[]{:S(2)}, u32[]{:S(2)}) async-start(f32[64,1,1664]{2,1,0:T(1,128)} %all_to_all.23), calls=%async_computation.2 | async-start | bytes 851968 | tf_op jit(solution)/shard_map/all_to_all | solution.py:17
  65.8 75.2 %all-gather.4.cloned.1.call-start = ((), (), s32[]{:S(2)}) async-start(), calls=%async_computation.4 | async-start | bytes 1671168 | tf_op jit(solution)/shard_map/all_gather | solution.py:49
  102.5 0.9 copy-start.3
  102.5 3.6 %copy-start.7 = (f32[1,2,96,128]{3,2,1,0:T(8,128)S(1)}, f32[1,2,96,128]{3,2,1,0:T(8,128)}, u32[]{:S(2)}) copy-start(f32[1,2,96,128]{3,2,1,0:T(8,128)} %param.17) | copy-start | bytes 294916
  102.5 3.6 %copy-start.8 = (f32[1,2,96,128]{3,2,1,0:T(8,128)S(1)}, f32[1,2,96,128]{3,2,1,0:T(8,128)}, u32[]{:S(2)}) copy-start(f32[1,2,96,128]{3,2,1,0:T(8,128)} %param.16) | copy-start | bytes 294916
  108.4 15.1 %all-to-all-start.3 = ((f32[32,16,128]{2,1,0:T(8,128)}), f32[32,16,128]{2,1,0:T(8,128)}, u32[]{:S(2)}, u32[]{:S(2)}) async-start(f32[32,16,128]{2,1,0:T(8,128)} %broadcast_in_dim.31), calls=%async_computation.3 | async-start | bytes 524288 | tf_op jit(solution)/shard_map/all_to_all | solution.py:17
  123.5 4.7 %copy-start.4 = (f32[42,1536]{1,0:T(8,128)S(1)}, f32[42,1536]{1,0:T(8,128)}, u32[]{:S(2)}) copy-start(f32[42,1536]{1,0:T(8,128)} %reshape.78) | copy-start | bytes 774148
  128.2 0.7 copy-start.5
  129.9 1.6 %copy-start.6 = (f32[42,1536]{1,0:T(8,128)S(1)}, f32[42,1536]{1,0:T(8,128)}, u32[]{:S(2)}) copy-start(f32[42,1536]{1,0:T(8,128)} %copy-done.5) | copy-start | bytes 774148
Sparse Core Ops, SparseCore 0:
  107.0 33.9 all-gather.3
where the time goes:
time: 152 us; the launch traced here: 151 us
  waiting for transfers between devices  53.4 us (35%)
  starting transfers between devices  35 us (23%)
  blocking collectives  19.7 us (13%)
  local copies, waits for them, and re-layouts  14.9 us (10%)
  between operations  14.4 us (9%)
  other arithmetic  7.52 us (5%)
  matrix products  6.02 us (4%)
    all_to_all x4, waiting for transfers between devices, exchange(): return lax.all_to_all(blocks, axes, 0, 0, tiled=True)  44.6 us
    all_to_all x4, starting transfers between devices, exchange(): return lax.all_to_all(blocks, axes, 0, 0, tiled=True)  35 us
    all_gather x1, blocking collectives, per_device(): bundle = lax.all_gather(bundle, 'shards', axis=0, tiled=False)  19.7 us
    all_gather x1, waiting for transfers between devices, per_device(): base = lax.all_gather(base_rows, 'shards', axis=1, tiled=True)  8.7 us
    broadcast_in_dim x1, other arithmetic, per_device(): new_weights = (base - step_size * approx)[None]  3.16 us
  transfers between devices with their start and end apart: 5, of which 5 were waited for; matrix products, arithmetic and copies ran while one was open for 10% of the time, Pallas kernels for 0%

commit v1 on v0

--- a/solution.py
+++ b/solution.py
@@ -46,7 +46,10 @@
     start = shard_index * rows
     blocks = width // lanes
     base_rows = weights[0] - step_size * momentum_decay * momentum[0]
-    base = lax.all_gather(base_rows, "shards", axis=1, tiled=True)
+    size = lax.axis_size("shards")
+    shards = jnp.stack([base_rows for _ in range(size)])
+    shards = lax.all_to_all(shards, "shards", split_axis=0, concat_axis=0)
+    base = jnp.concatenate(shards, axis=1)
     columns = jnp.concatenate([router_partials[0].T, gain_partials[0]], 0).astype(f32)
     count = columns.shape[0]
     strips = columns.reshape(count, blocks, lanes).transpose(1, 0, 2).reshape(count * blocks, lanes)

time: 152 us -> 162 us (1.066)
  waiting for transfers between devices: 53.4 us -> 69.3 us
  between operations: 14.4 us -> 1.03 us
  starting transfers between devices: 35 us -> 40.4 us
  local copies, waits for them, and re-layouts: 14.9 us -> 17 us
    all_to_all x0 -> x1, waiting for transfers between devices: none -> 27.8 us  [per_device(): shards = lax.all_to_all(shards, 'shards', split_axis=0, concat_axis=0)]
    all_gather x1 -> x0, waiting for transfers between devices: 8.7 us -> none  [per_device(): base = lax.all_gather(base_rows, 'shards', axis=1, tiled=True)]
    all_to_all x0 -> x1, starting transfers between devices: none -> 6.13 us  [per_device(): shards = lax.all_to_all(shards, 'shards', split_axis=0, concat_axis=0)]
    broadcast_in_dim x1 -> x0, other arithmetic: 3.16 us -> none  [per_device(): new_weights = (base - step_size * approx)[None]]
    all_to_all x4, waiting for transfers between devices: 44.6 us -> 41.5 us  [exchange(): return lax.all_to_all(blocks, axes, 0, 0, tiled=True)]
  transfers between devices with their start and end apart: 5 -> 5, of which waited for: 5 -> 5; matrix products, arithmetic and copies ran while one was open for 10% -> 12% of each run, Pallas kernels for 0% -> 0%
where the time goes in v1:
time: 162 us; the launch traced here: 161 us
  waiting for transfers between devices  69.3 us (43%)
  starting transfers between devices  40.4 us (25%)
  blocking collectives  19.7 us (12%)
  local copies, waits for them, and re-layouts  17 us (10%)
  other arithmetic  7.11 us (4%)
  matrix products  7.02 us (4%)
    all_to_all x4, waiting for transfers between devices, exchange(): return lax.all_to_all(blocks, axes, 0, 0, tiled=True)  41.5 us
    all_to_all x4, starting transfers between devices, exchange(): return lax.all_to_all(blocks, axes, 0, 0, tiled=True)  34.2 us
    all_to_all x1, waiting for transfers between devices, per_device(): shards = lax.all_to_all(shards, 'shards', split_axis=0, concat_axis=0)  27.8 us
    all_gather x1, blocking collectives, per_device(): bundle = lax.all_gather(bundle, 'shards', axis=0, tiled=False)  19.7 us
    all_to_all x1, starting transfers between devices, per_device(): shards = lax.all_to_all(shards, 'shards', split_axis=0, concat_axis=0)  6.13 us
    dot_general x1, matrix products, per_device(): approx = jnp.einsum('ktd,ktf->kdf', p_hat, q_avg, precision=highest)  3.62 us
  transfers between devices with their start and end apart: 5, of which 5 were waited for; matrix products, arithmetic and copies ran while one was open for 12% of the time, Pallas kernels for 0%

profile of v1, /device:TPU:1, one launch (start us, length us, event | category | flops | bytes accessed | tf_op | source)
XLA Modules:
  0.0 161.5 jit_solution(18408578012392421334)
XLA Ops:
  3.4 7.7 %all-to-all-start.1 = ((f32[8,64,128]{2,1,0:T(8,128)}), f32[8,64,128]{2,1,0:T(8,128)S(1)}, u32[]{:S(2)}, u32[]{:S(2)}) async-start(f32[8,64,128]{2,1,0:T(8,128)} %copy.30), calls=%async_computation.1 | async-start | bytes 524288 | tf_op jit(solution)/shard_map/all_to_all | solution.py:17
  11.1 1.8 %fusion.2 = f32[2,1536,32]{1,2,0:T(8,128)S(1)} fusion(bf16[1,1,2,1536,128]{4,3,2,1,0:T(8,128)(2,1)S(1)} %copy-done.1, bf16[1,1,2,1536,128]{4,3,2,1,0:T(8,128)(2,1)S(1)} %copy-done.2, f32[1,2,128,32]{2,3,1,0:T(8,128)S(1)} %copy-done), kind=kOutput, calls=%fused_computation.4 | convolution fusion | flops 152174592 | bytes 1998848 | tf_op jit(solution)/shard_map/krf,kdf->krd/dot_general | solution.py:63
  12.9 1.2 copy.27
  14.1 6.4 %all-to-all-done.1 = f32[8,64,128]{2,1,0:T(8,128)S(1)} async-done(((f32[8,64,128]{2,1,0:T(8,128)}), f32[8,64,128]{2,1,0:T(8,128)S(1)}, u32[]{:S(2)}, u32[]{:S(2)}) %all-to-all-start.1) | async-done | bytes 262176 | tf_op jit(solution)/shard_map/all_to_all | solution.py:17
  20.5 16.8 %all-to-all-start = ((f32[64,1,1536]{2,1,0:T(1,128)}), f32[64,1,1536]{2,1,0:T(1,128)S(1)}, u32[]{:S(2)}, u32[]{:S(2)}) async-start(f32[64,1,1536]{2,1,0:T(1,128)} %copy.27), calls=%async_computation | async-start | bytes 786432 | tf_op jit(solution)/shard_map/all_to_all | solution.py:17
  37.3 14.6 %all-to-all-done = f32[64,1,1536]{2,1,0:T(1,128)S(1)} async-done(((f32[64,1,1536]{2,1,0:T(1,128)}), f32[64,1,1536]{2,1,0:T(1,128)S(1)}, u32[]{:S(2)}, u32[]{:S(2)}) %all-to-all-start) | async-done | bytes 393248 | tf_op jit(solution)/shard_map/all_to_all | solution.py:17
  52.2 1.1 all_to_all.26
  53.2 6.0 %all-to-all-start.2 = ((f32[64,1,1664]{2,1,0:T(1,128)}), f32[64,1,1664]{2,1,0:T(1,128)S(1)}, u32[]{:S(2)}, u32[]{:S(2)}) async-start(f32[64,1,1664]{2,1,0:T(1,128)} %all_to_all.26), calls=%async_computation.2 | async-start | bytes 851968 | tf_op jit(solution)/shard_map/all_to_all | solution.py:17
  59.3 15.3 %all-to-all-done.2 = f32[64,1,1664]{2,1,0:T(1,128)S(1)} async-done(((f32[64,1,1664]{2,1,0:T(1,128)}), f32[64,1,1664]{2,1,0:T(1,128)S(1)}, u32[]{:S(2)}, u32[]{:S(2)}) %all-to-all-start.2) | async-done | bytes 426016 | tf_op jit(solution)/shard_map/all_to_all | solution.py:17
  75.2 1.1 fusion
  76.3 19.7 %all-gather = f32[1920,128]{1,0:T(8,128)S(1)} all-gather(f32[120,128]{1,0:T(8,128)S(1)} %select_maximum_fusion), channel_id=2, replica_groups=mesh['shards'=16,'tensor'=4,'sections'=8] {'shards'}, dimensions={0}, use_global_device_ids=true | all-gather | bytes 1044480 | tf_op jit(solution)/shard_map/all_gather | solution.py:82
  97.7 3.9 %all-to-all-start.4 = ((f32[32,16,128]{2,1,0:T(8,128)}), f32[32,16,128]{2,1,0:T(8,128)S(1)}, u32[]{:S(2)}, u32[]{:S(2)}) async-start(f32[32,16,128]{2,1,0:T(8,128)} %broadcast_in_dim.31), calls=%async_computation.4 | async-start | bytes 524288 | tf_op jit(solution)/shard_map/all_to_all | solution.py:17
  101.6 3.6 %fusion.10 = f32[2,1536,128]{2,1,0:T(8,128)S(1)} fusion(f32[2,1536,32]{1,2,0:T(8,128)} %copy-done.4, f32[2,32,128]{2,1,0:T(8,128)S(1)} %bitcast.91), kind=kOutput, calls=%fused_computation.35 | convolution fusion | flops 150994944 | bytes 1998848 | tf_op jit(solution)/shard_map/ktd,ktf->kdf/dot_general | solution.py:93
  105.2 1.6 subtract_bitcast_fusion
  106.8 5.2 %all-to-all-done.4 = f32[32,16,128]{2,1,0:T(8,128)S(1)} async-done(((f32[32,16,128]{2,1,0:T(8,128)}), f32[32,16,128]{2,1,0:T(8,128)S(1)}, u32[]{:S(2)}, u32[]{:S(2)}) %all-to-all-start.4) | async-done | bytes 262176 | tf_op jit(solution)/shard_map/all_to_all | solution.py:17
  112.1 1.3 stack.5
  113.4 6.1 %all-to-all-start.3 = ((f32[16,2,96,128]{3,2,1,0:T(8,128)}), f32[16,2,96,128]{3,2,1,0:T(8,128)}, u32[]{:S(2)}, u32[]{:S(2)}) async-start(f32[16,2,96,128]{3,2,1,0:T(8,128)} %stack.5), calls=%async_computation.3 | async-start | bytes 3145728 | tf_op jit(solution)/shard_map/all_to_all | solution.py:51
  119.5 1.0 slice.45
  121.6 1.8 %slice_multiply_fusion.1 = (f32[504,128]{1,0:T(8,128)}, f32[504,128]{1,0:T(8,128)}) fusion(f32[512,128]{1,0:T(8,128)} %bitcast.87), kind=kLoop, calls=%fused_computation.15 | loop fusion | flops 129024 | bytes 774144 | tf_op jit(solution)/shard_map/mul | solution.py:101
  123.4 1.7 %mul.77 = f32[12,42,128]{2,1,0:T(8,128)} reshape(f32[504,128]{1,0:T(8,128)} %get-tuple-element.9) | data formatting | bytes 516096 | tf_op jit(solution)/shard_map/mul | solution.py:101
  125.1 1.1 copy.35
  130.3 27.8 %all-to-all-done.3 = f32[16,2,96,128]{3,2,1,0:T(8,128)} async-done(((f32[16,2,96,128]{3,2,1,0:T(8,128)}), f32[16,2,96,128]{3,2,1,0:T(8,128)}, u32[]{:S(2)}, u32[]{:S(2)}) %all-to-all-start.3) | async-done | bytes 1572896 | tf_op jit(solution)/shard_map/all_to_all | solution.py:51
  158.1 1.5 copy.32
  159.7 1.8 %bitcast_subtract_fusion = (f32[2,1536,128]{2,1,0:T(8,128)}, bf16[1,1,2,1536,128]{4,3,2,1,0:T(8,128)(2,1)}) fusion(f32[2,16,96,128]{3,2,1,0:T(8,128)S(1)} %copy.32, f32[2,1536,128]{2,1,0:T(8,128)S(1)} %fusion.10, bf16[1,1,2,1536,128]{4,3,2,1,0:T(8,128)(2,1)S(1)} %copy-done.1, bf16[1,1,2,1536,128]{4,3,2,1,0:T(8,128)(2,1)S(1)} %copy-done.2), kind=kLoop, calls=%fused_computation | loop fusion | flops 2752512 | bytes 7077888 | tf_op jit(solution)/shard_map/sub | solution.py:95
  (67 shorter events, 10.6 us)
Async XLA Ops:
  0.6 10.5 %copy-start = (f32[1,2,128,32]{2,3,1,0:T(8,128)S(1)}, f32[1,2,128,32]{2,3,1,0:T(8,128)}, u32[]{:S(2)}) copy-start(f32[1,2,128,32]{2,3,1,0:T(8,128)} %param.14) | copy-start | bytes 98308
  0.6 10.4 %copy-start.1 = (bf16[1,1,2,1536,128]{4,3,2,1,0:T(8,128)(2,1)S(1)}, bf16[1,1,2,1536,128]{4,3,2,1,0:T(8,128)(2,1)}, u32[]{:S(2)}) copy-start(bf16[1,1,2,1536,128]{4,3,2,1,0:T(8,128)(2,1)} %param.13) | copy-start | bytes 2359300
  0.7 10.4 %copy-start.2 = (bf16[1,1,2,1536,128]{4,3,2,1,0:T(8,128)(2,1)S(1)}, bf16[1,1,2,1536,128]{4,3,2,1,0:T(8,128)(2,1)}, u32[]{:S(2)}) copy-start(bf16[1,1,2,1536,128]{4,3,2,1,0:T(8,128)(2,1)} %param.12) | copy-start | bytes 2359300
  3.4 17.1 %all-to-all-start.1 = ((f32[8,64,128]{2,1,0:T(8,128)}), f32[8,64,128]{2,1,0:T(8,128)S(1)}, u32[]{:S(2)}, u32[]{:S(2)}) async-start(f32[8,64,128]{2,1,0:T(8,128)} %copy.30), calls=%async_computation.1 | async-start | bytes 524288 | tf_op jit(solution)/shard_map/all_to_all | solution.py:17
  20.5 31.4 %all-to-all-start = ((f32[64,1,1536]{2,1,0:T(1,128)}), f32[64,1,1536]{2,1,0:T(1,128)S(1)}, u32[]{:S(2)}, u32[]{:S(2)}) async-start(f32[64,1,1536]{2,1,0:T(1,128)} %copy.27), calls=%async_computation | async-start | bytes 786432 | tf_op jit(solution)/shard_map/all_to_all | solution.py:17
  37.3 22.0 %copy-start.13 = (f32[2,96]{1,0:T(2,128)S(1)}, f32[2,96]{1,0:T(2,128)}, u32[]{:S(2)}) copy-start(f32[2,96]{1,0:T(2,128)} %param.22) | copy-start | bytes 2308
  37.3 22.0 %copy-start.14 = (f32[2,96]{1,0:T(2,128)S(1)}, f32[2,96]{1,0:T(2,128)}, u32[]{:S(2)}) copy-start(f32[2,96]{1,0:T(2,128)} %param.23) | copy-start | bytes 2308
  37.3 22.0 %copy-start.9 = (f32[96,40]{0,1:T(8,128)S(1)}, f32[96,40]{0,1:T(8,128)}, u32[]{:S(2)}) copy-start(f32[96,40]{0,1:T(8,128)} %param.20) | copy-start | bytes 46084
  37.3 22.0 %copy-start.12 = (f32[96,40]{0,1:T(8,128)S(1)}, f32[96,40]{0,1:T(8,128)}, u32[]{:S(2)}) copy-start(f32[96,40]{0,1:T(8,128)} %param.21) | copy-start | bytes 46084
  52.2 22.5 %copy-start.11 = (f32[1,2,32,32]{3,2,1,0:T(8,128)S(1)}, f32[1,2,32,32]{3,2,1,0:T(8,128)}, u32[]{:S(2)}) copy-start(f32[1,2,32,32]{3,2,1,0:T(8,128)} %param.15) | copy-start | bytes 24580
  53.2 21.4 %all-to-all-start.2 = ((f32[64,1,1664]{2,1,0:T(1,128)}), f32[64,1,1664]{2,1,0:T(1,128)S(1)}, u32[]{:S(2)}, u32[]{:S(2)}) async-start(f32[64,1,1664]{2,1,0:T(1,128)} %all_to_all.26), calls=%async_computation.2 | async-start | bytes 851968 | tf_op jit(solution)/shard_map/all_to_all | solution.py:17
  75.2 20.8 %copy-start.4 = (f32[2,1536,32]{1,2,0:T(8,128)}, f32[2,1536,32]{1,2,0:T(8,128)S(1)}, u32[]{:S(2)}) copy-start(f32[2,1536,32]{1,2,0:T(8,128)S(1)} %fusion.6) | copy-start | bytes 1179652
  96.0 1.0 copy-start.3
  97.7 14.4 %all-to-all-start.4 = ((f32[32,16,128]{2,1,0:T(8,128)}), f32[32,16,128]{2,1,0:T(8,128)S(1)}, u32[]{:S(2)}, u32[]{:S(2)}) async-start(f32[32,16,128]{2,1,0:T(8,128)} %broadcast_in_dim.31), calls=%async_computation.4 | async-start | bytes 524288 | tf_op jit(solution)/shard_map/all_to_all | solution.py:17
  112.1 1.3 copy-start.8
  113.4 44.7 %all-to-all-start.3 = ((f32[16,2,96,128]{3,2,1,0:T(8,128)}), f32[16,2,96,128]{3,2,1,0:T(8,128)}, u32[]{:S(2)}, u32[]{:S(2)}) async-start(f32[16,2,96,128]{3,2,1,0:T(8,128)} %stack.5), calls=%async_computation.3 | async-start | bytes 3145728 | tf_op jit(solution)/shard_map/all_to_all | solution.py:51
  121.6 4.7 %copy-start.5 = (f32[42,1536]{1,0:T(8,128)S(1)}, f32[42,1536]{1,0:T(8,128)}, u32[]{:S(2)}) copy-start(f32[42,1536]{1,0:T(8,128)} %reshape.84) | copy-start | bytes 774148
  126.3 2.6 %copy-start.10 = (f32[96,40]{0,1:T(8,128)S(1)}, f32[96,40]{0,1:T(8,128)}, u32[]{:S(2)}) copy-start(f32[96,40]{0,1:T(8,128)} %param.20) | copy-start | bytes 46084
  126.4 0.7 copy-start.6
  128.0 1.6 copy-start.7
